TPU v7x, 256 devices: a whole 4x4x8 slice. The times are simulated.
256 devices in a mesh: seq: 32 (over z, x), head: 8 (over y, core).
Axes of the slice: x: 4, y: 4, z: 8, core: 2. Of those that a mesh axis runs over, the one named last changes fastest.
Arguments:
- block_input: bfloat16 [8, 256, 5120], P(None, 'seq'), may hold values from -6 to 6
- accepted: bfloat16 [8, 256, 5120], P(None, 'seq'), may hold values from -6 to 6
- accept_mask: int32 [8, 256], P(None, 'seq'), may hold values 0 or 1
- cache_lengths: int32 [8], replicated, may hold values from 1 to 8192, as said below
- page_table: int32 [512], replicated, may hold values from 0 to 511, each once
- norm_gain: float32 [5120], replicated, may hold values from 0.1 to 1.9
- w_query: bfloat16 [5120, 3072], P('seq', 'head'), may hold values from -0.078125 to 0.078125
- w_key: bfloat16 [5120, 3072], P('seq', 'head'), may hold values from -0.078125 to 0.078125
- w_value: bfloat16 [5120, 3072], P('seq', 'head'), may hold values from -0.25 to 0.25
- w_out: bfloat16 [5120, 3072], P('seq', 'head'), may hold values from -0.109375 to 0.109375
- key_cache: bfloat16 [512, 128, 3072], P('seq', None, 'head')
- value_cache: bfloat16 [512, 128, 3072], P('seq', None, 'head'), may hold values from -18 to 18
Outputs:
- first_out: bfloat16 [8, 256, 5120], P(None, 'seq', 'head')
- second_out: bfloat16 [8, 256, 5120], P(None, 'seq', 'head')
Inputs may be any that keep to these rules, and one draw needn't show every extreme that they name: `cache_lengths`: max(1, 4) requests, chosen at random, hold (63) * 128 + 1 to 8192 cached tokens, one of them exactly 8192; the others hold 1 to 256. `page_table`: A permutation of the 512 pool pages; entry r * 64 + j is the pool page of cached positions j * 128 to (j + 1) * 128 - 1 of request r.
All inputs are finite; a program needn't handle non-finite values. No bound on the sum of `accept_mask` on one device may be relied on, other than what follows from the above.
Results may differ from a plain program's by a relative error of at most 0.024.
The roundings to bfloat16 on the way count: a program that leaves them out, or rounds other values in their place, can miss the bound.
Values may be sent and summed in bfloat16 or wider, within the bound.
A program may use at most 128 MiB of HBM per device.

v0:
```python
import jax
import jax.numpy as jnp
from jax import lax
from jax.sharding import PartitionSpec as P

HD = 128
PAGE = 128
MAXP = 64
masked_score = -1e30


def rotate(vectors, positions):
    half_width = vectors.shape[-1] // 2
    frequency = 10000.0 ** (-(jnp.arange(half_width).astype(jnp.float32) * 2.0) / vectors.shape[-1])
    angles = positions[..., None, None] * frequency
    cosine = jnp.cos(angles)
    sine_part = jnp.sin(angles)
    front_half = vectors[..., :half_width]
    back_half = vectors[..., half_width:]
    return jnp.concatenate(
        [front_half * cosine - back_half * sine_part, back_half * cosine + front_half * sine_part],
        axis=-1,
    )


def normalize(inputs, norm_gain):
    widened = inputs.astype(jnp.float32)
    inverse = lax.rsqrt(jnp.mean(widened * widened, axis=-1, keepdims=True) + 1e-05)
    return (widened * inverse * norm_gain).astype(jnp.bfloat16)


def per_device(
    block_input,
    accepted,
    accept_mask,
    cache_lengths,
    page_table,
    norm_gain,
    w_query,
    w_key,
    w_value,
    w_out,
    key_cache,
    value_cache,
):
    seq_place = lax.axis_index("seq")
    requests, part_len, model_width = block_input.shape
    local_width = w_query.shape[1]
    local_heads = local_width // HD
    row_count = 2 * requests * part_len
    swapped = jnp.where(accept_mask[:, :, None] == 1, accepted, block_input)
    token_rows = normalize(jnp.stack([block_input, swapped]), norm_gain).reshape(
        row_count, model_width
    )
    full_query, full_key, full_value, out_weight = (
        lax.all_gather(w_query, "seq", axis=0, tiled=True),
        lax.all_gather(w_key, "seq", axis=0, tiled=True),
        lax.all_gather(w_value, "seq", axis=0, tiled=True),
        lax.all_gather(w_out, "seq", axis=0, tiled=True),
    )
    query_rows = jnp.dot(token_rows, full_query, preferred_element_type=jnp.float32)
    key_rows = jnp.dot(token_rows, full_key, preferred_element_type=jnp.float32)
    value_rows = jnp.dot(token_rows, full_value, preferred_element_type=jnp.float32)
    positions = (
        cache_lengths[:, None]
        + seq_place * part_len
        + jnp.arange(part_len, dtype=jnp.int32)[None, :]
    ).astype(jnp.float32)
    shaped = (2, requests, part_len, local_heads, HD)
    new_queries = rotate(query_rows.reshape(shaped), positions).astype(jnp.bfloat16)
    new_keys = rotate(key_rows.reshape(shaped), positions).astype(jnp.bfloat16)
    new_values = value_rows.reshape(shaped).astype(jnp.bfloat16)
    every_query = lax.all_gather(new_queries, "seq", axis=2, tiled=True)
    pages_here = key_cache.shape[0]
    page_ids = seq_place * pages_here + jnp.arange(pages_here, dtype=jnp.int32)
    table_slots = jnp.arange(page_table.shape[0], dtype=jnp.int32)
    slot_of = jnp.sum(
        jnp.where(page_table[None, :] == page_ids[:, None], table_slots[None, :], 0), axis=1
    )
    page_owner = slot_of // MAXP
    owner_match = page_owner[:, None] == jnp.arange(requests, dtype=jnp.int32)[None, :]
    owner_length = jnp.sum(jnp.where(owner_match, cache_lengths[None, :], 0), axis=1)
    offsets = (slot_of % MAXP)[:, None] * PAGE + jnp.arange(PAGE, dtype=jnp.int32)[None, :]
    live_mask = (offsets < owner_length[:, None])[:, None, None, :]
    owner_hot = owner_match.astype(jnp.float32)
    cached_keys = key_cache.reshape(pages_here, PAGE, local_heads, HD)
    cached_values = value_cache.reshape(pages_here, PAGE, local_heads, HD)
    score_scale = HD ** (-0.5)

    def local_part(pass_items):
        pass_queries, pass_keys, pass_values = pass_items
        page_queries = jnp.take(pass_queries, page_owner, axis=0)
        scores = (
            jnp.einsum(
                "pqhd,pkhd->pqhk", page_queries, cached_keys, preferred_element_type=jnp.float32
            )
            * score_scale
        )
        scores = jnp.where(live_mask, scores, masked_score)
        page_peak = jnp.max(scores, axis=-1)
        weights = jnp.where(live_mask, jnp.exp(scores - page_peak[..., None]), 0.0)
        page_total = jnp.sum(weights, axis=-1)
        page_out = jnp.einsum(
            "pqhk,pkhd->pqhd",
            weights.astype(jnp.bfloat16),
            cached_values,
            preferred_element_type=jnp.float32,
        )
        owner_peak = jnp.max(
            jnp.where(owner_match[:, :, None, None], page_peak[:, None], masked_score), axis=0
        )
        factor = jnp.exp(page_peak - jnp.take(owner_peak, page_owner, axis=0))
        cache_total = jnp.einsum(
            "pr,pqh->rqh", owner_hot, page_total * factor, precision=lax.Precision.HIGHEST
        )
        cache_out = jnp.einsum(
            "pr,pqhd->rqhd",
            owner_hot,
            page_out * factor[..., None],
            precision=lax.Precision.HIGHEST,
        )
        block_scores = (
            jnp.einsum(
                "rqhd,rkhd->rqhk", pass_queries, pass_keys, preferred_element_type=jnp.float32
            )
            * score_scale
        )
        block_peak = jnp.max(block_scores, axis=-1)
        block_weights = jnp.exp(block_scores - block_peak[..., None])
        block_total = jnp.sum(block_weights, axis=-1)
        block_out = jnp.einsum(
            "rqhk,rkhd->rqhd",
            block_weights,
            pass_values.astype(jnp.float32),
            precision=lax.Precision.HIGHEST,
        )
        row_peak = jnp.maximum(owner_peak, block_peak)
        cache_factor = jnp.exp(owner_peak - row_peak)
        block_factor = jnp.exp(block_peak - row_peak)
        joined_total = cache_total * cache_factor + block_total * block_factor
        joined_out = cache_out * cache_factor[..., None] + block_out * block_factor[..., None]
        return (row_peak, joined_total, joined_out)

    row_peak, row_total, row_out = lax.map(local_part, (every_query, new_keys, new_values))
    overall = lax.pmax(row_peak, "seq")
    rescale = jnp.exp(row_peak - overall)
    summed_out, summed_total = (
        lax.psum_scatter(row_out * rescale[..., None], "seq", scatter_dimension=2, tiled=True),
        lax.psum_scatter(row_total * rescale, "seq", scatter_dimension=2, tiled=True),
    )
    context = (
        (summed_out / summed_total[..., None]).astype(jnp.bfloat16).reshape(row_count, local_width)
    )
    partial_value = lax.dot_general(
        context, out_weight, (((1,), (1,)), ((), ())), preferred_element_type=jnp.float32
    )
    own_share = lax.psum_scatter(partial_value, "head", scatter_dimension=1, tiled=True).astype(
        jnp.bfloat16
    )
    result = own_share.reshape(2, requests, part_len, own_share.shape[1])
    return (result[0], result[1])


def solution(mesh):
    placed = (
        P(None, "seq", None),
        P(None, "seq", None),
        P(None, "seq"),
        P(),
        P(),
        P(),
        P("seq", "head"),
        P("seq", "head"),
        P("seq", "head"),
        P("seq", "head"),
        P("seq", None, "head"),
        P("seq", None, "head"),
    )
    return jax.shard_map(
        per_device,
        mesh=mesh,
        in_specs=placed,
        out_specs=(P(None, "seq", "head"), P(None, "seq", "head")),
        check_vma=False,
    )
```

profile of v0, /device:TPU:2, one launch (start us, length us, event | category | flops | bytes accessed | tf_op | source)
XLA Modules:
  0.0 919.2 jit_solution(8133665721481068145)
XLA Ops:
  13.3 80.1 %all-gather.10.cloned.1.call-done = bf16[5120,384]{1,0:T(8,128)(2,1)} async-done(((bf16[160,384]{1,0:T(8,128)(2,1)}), bf16[5120,384]{1,0:T(8,128)(2,1)}) %all-gather.10.cloned.1.call-update) | async-done | bytes 3932176 | tf_op jit(solution)/shard_map/all_gather | solution.py:57
  93.4 6.3 copy.77
  99.7 74.6 %all-gather.6.cloned.1.call-done = bf16[5120,384]{1,0:T(8,128)(2,1)} async-done(((bf16[160,384]{1,0:T(8,128)(2,1)}), bf16[5120,384]{1,0:T(8,128)(2,1)}) %all-gather.6.cloned.1.call-update) | async-done | bytes 3932176 | tf_op jit(solution)/shard_map/all_gather | solution.py:56
  174.3 6.3 copy.75
  180.6 3.5 fusion.59
  193.9 61.3 %all-gather.12.cloned.1.call-done = bf16[5120,384]{1,0:T(8,128)(2,1)} async-done(((bf16[160,384]{1,0:T(8,128)(2,1)}), bf16[5120,384]{1,0:T(8,128)(2,1)}) %all-gather.12.cloned.1.call-update) | async-done | bytes 3932176 | tf_op jit(solution)/shard_map/all_gather | solution.py:58
  255.2 6.3 copy.79
  262.2 4.0 convolution_convert_fusion
  266.2 69.3 %all-gather.8.cloned.1.call-done = bf16[2,8,256,3,128]{4,2,3,1,0:T(8,128)(2,1)} async-done(((bf16[2,8,8,3,128]{4,2,3,1,0:T(8,128)(2,1)}), bf16[2,8,256,3,128]{4,2,3,1,0:T(8,128)(2,1)}) %all-gather.8.cloned.1.call-update) | async-done | bytes 3145744 | tf_op jit(solution)/shard_map/all_gather | solution.py:73
  335.5 82.3 %while.16 = (s32[]{:T(128)}, f32[2,8,256,3]{2,1,3,0:T(8,128)}, f32[2,8,256,3]{2,1,3,0:T(8,128)}, f32[2,8,256,3,128]{4,2,3,1,0:T(8,128)}, s32[16]{0:T(128)S(1)}, ...) while((s32[]{:T(128)}, f32[2,8,256,3]{2,1,3,0:T(8,128)}, ...), condition=%wide.region_9.10_spmd.clone.clone, body=%wide.region_3.9_spmd.clone.clone.sunk | while | flops 1071998720 | bytes 124305208 | solution.py:144
  337.0 2.7 gather_fusion
  339.8 3.0 bitcast_reduce_fusion.2
  346.8 8.2 bitcast_multiply_fusion.4
  362.2 11.2 %fusion.103 = f32[1,8,256,3,128]{4,1,3,2,0:T(8,128)S(1)} fusion(f32[8,3,128,256]{2,0,1,3:T(8,128)} %copy.126, f32[16,256,3,128]{3,1,2,0:T(8,128)} %bitcast_multiply_fusion.4, f32[8,256,3]{0,2,1:T(4,128)} %copy.127, f32[8,256,3]{0,2,1:T(4,128)} %copy.128, s32[16]{0:T(128)S(1)} %get-tuple-element.340), kind=kOutput, calls=%fused_computation.19.clone.1 | convolution fusion | flops 153354496 | bytes 12632128 | tf_op jit(solution)/shard_map/while/body/eval_jaxpr/pr,pqhd->rqhd/dot_general | solution.py:116
  380.9 3.0 bitcast_reduce_fusion.2
  387.9 8.2 bitcast_multiply_fusion.4
  403.4 11.2 %fusion.103 = f32[1,8,256,3,128]{4,1,3,2,0:T(8,128)S(1)} fusion(f32[8,3,128,256]{2,0,1,3:T(8,128)} %copy.126, f32[16,256,3,128]{3,1,2,0:T(8,128)} %bitcast_multiply_fusion.4, f32[8,256,3]{0,2,1:T(4,128)} %copy.127, f32[8,256,3]{0,2,1:T(4,128)} %copy.128, s32[16]{0:T(128)S(1)} %get-tuple-element.340), kind=kOutput, calls=%fused_computation.19.clone.1 | convolution fusion | flops 153354496 | bytes 12632128 | tf_op jit(solution)/shard_map/while/body/eval_jaxpr/pr,pqhd->rqhd/dot_general | solution.py:116
  417.8 137.8 %pmax.7 = f32[2,8,256,3]{2,1,3,0:T(8,128)S(1)} all-reduce(f32[2,8,256,3]{2,1,3,0:T(8,128)} %get-tuple-element.72), channel_id=1, replica_groups=mesh['seq'=32,'head'=8] {'seq'}, use_global_device_ids=true, to_apply=%region_10.11 | all-reduce | flops 12288 | bytes 98304 | tf_op jit(solution)/shard_map/pmax | solution.py:145
  556.5 7.3 broadcast_multiply_fusion
  565.7 140.1 %all-reduce = f32[2,8,256,3]{2,1,3,0:T(8,128)S(1)} all-reduce(f32[2,8,256,3]{2,1,3,0:T(8,128)S(1)} %get-tuple-element.201), channel_id=3, replica_groups=mesh['seq'=32,'head'=8] {'seq'}, use_global_device_ids=true, to_apply=%region_12.13.clone | all-reduce | flops 12288 | bytes 98304
  706.0 82.0 %reduce-scatter.4.cloned.1.call-done = f32[2,8,8,3,128]{4,2,3,1,0:T(8,128)} async-done(((f32[2,8,256,3,128]{4,2,3,1,0:T(8,128)}), f32[2,8,8,3,128]{4,2,3,1,0:T(8,128)}) %reduce-scatter.4.cloned.1.call-update) | async-done | bytes 196624 | tf_op jit(solution)/shard_map/reduce_scatter | solution.py:148
  789.1 80.8 %all-gather.14.cloned.1.call-done = bf16[5120,384]{1,0:T(8,128)(2,1)} async-done(((bf16[160,384]{1,0:T(8,128)(2,1)}), bf16[5120,384]{1,0:T(8,128)(2,1)}) %all-gather.14.cloned.1.call-update) | async-done | bytes 3932176 | tf_op jit(solution)/shard_map/all_gather | solution.py:59
  869.8 5.0 fusion.66
  874.8 35.8 %reduce-scatter.6.cloned.1.call-done = f32[128,640]{1,0:T(8,128)} async-done(((f32[128,5120]{1,0:T(8,128)}), f32[128,640]{1,0:T(8,128)}) %reduce-scatter.6.cloned.1.call-update) | async-done | bytes 327696 | tf_op jit(solution)/shard_map/reduce_scatter | solution.py:157
  (136 shorter events, 55.7 us)
Async XLA Ops:
  7.2 5.8 copy-start.13
  7.2 86.2 %all-gather.10.cloned.1.call-start = ((), (), s32[]{:S(2)}) async-start(), calls=%async_computation.4 | async-start | bytes 4055040 | tf_op jit(solution)/shard_map/all_gather | solution.py:57
  7.9 166.4 %all-gather.6.cloned.1.call-start = ((), (), s32[]{:S(2)}) async-start(), calls=%async_computation.2 | async-start | bytes 4055040 | tf_op jit(solution)/shard_map/all_gather | solution.py:56
  8.7 246.5 %all-gather.12.cloned.1.call-start = ((), (), s32[]{:S(2)}) async-start(), calls=%async_computation.5 | async-start | bytes 4055040 | tf_op jit(solution)/shard_map/all_gather | solution.py:58
  9.4 326.1 %all-gather.8.cloned.1.call-start = ((), (), s32[]{:S(2)}) async-start(), calls=%async_computation.3 | async-start | bytes 3244032 | tf_op jit(solution)/shard_map/all_gather | solution.py:73
  174.3 6.3 copy-start.3
  174.3 6.3 copy-start.12
  180.6 3.5 copy-start.2
  186.4 601.6 %reduce-scatter.4.cloned.1.call-start = ((), (), s32[]{:S(2)}) async-start(), calls=%async_computation.6 | async-start | bytes 6488064 | tf_op jit(solution)/shard_map/reduce_scatter | solution.py:148
  190.0 3.6 copy-start.11
  337.0 2.8 copy-start.4
  342.8 2.6 copy-start
  346.8 8.2 copy-start.1
  346.8 8.2 copy-start.6
  373.4 2.3 copy-start.9
  373.4 2.5 copy-start.7
  378.2 2.8 copy-start.4
  383.9 2.6 copy-start
  387.9 8.3 copy-start.1
  387.9 8.3 copy-start.6
  414.6 2.4 copy-start.9
  414.6 2.6 copy-start.7
  563.9 306.0 %all-gather.14.cloned.1.call-start = ((), (), s32[]{:S(2)}) async-start(), calls=%async_computation.7 | async-start | bytes 4055040 | tf_op jit(solution)/shard_map/all_gather | solution.py:59
  564.4 346.2 %reduce-scatter.6.cloned.1.call-start = ((), (), s32[]{:S(2)}) async-start(), calls=%async_computation.8 | async-start | bytes 2949120 | tf_op jit(solution)/shard_map/reduce_scatter | solution.py:157
  (7 other events, 6.0 us)
Sparse Core Ops, SparseCore 0:
  10.6 82.7 all-gather.9
  96.0 78.2 all-gather.5
  176.9 78.2 all-gather.11
  257.5 77.9 all-gather.7
  564.0 223.9 reduce-scatter.3
  790.8 79.0 all-gather.13
  874.9 35.6 reduce-scatter.5
where the time goes:
time: 920 us; the launch traced here: 919 us
  waiting for transfers between devices  487 us (53%)
  blocking collectives  278 us (30%)
  matrix products  64.6 us (7%)
  local copies, waits for them, and re-layouts  53.1 us (6%)
  other arithmetic  21.4 us (2%)
  between operations  14.9 us (2%)
    unnamed x1, blocking collectives  140 us
    pmax x1, blocking collectives, per_device(): overall = lax.pmax(row_peak, 'seq')  138 us
    reduce_scatter x1, waiting for transfers between devices, per_device(): lax.psum_scatter(row_out * rescale[..., None], 'seq', scatter_dimension=2...  82 us
    all_gather x1, waiting for transfers between devices, per_device(): lax.all_gather(w_out, 'seq', axis=0, tiled=True)  80.8 us
    all_gather x1, waiting for transfers between devices, per_device(): lax.all_gather(w_key, 'seq', axis=0, tiled=True)  80.1 us
    all_gather x1, waiting for transfers between devices, per_device(): lax.all_gather(w_query, 'seq', axis=0, tiled=True)  74.6 us
    all_gather x1, waiting for transfers between devices, per_device(): every_query = lax.all_gather(new_queries, 'seq', axis=2, tiled=True)  69.3 us
    all_gather x1, waiting for transfers between devices, per_device(): lax.all_gather(w_value, 'seq', axis=0, tiled=True)  61.3 us
  transfers between devices with their start and end apart: 7, of which 7 were waited for; matrix products, arithmetic and copies ran while one was open for 5% of the time, Pallas kernels for 0%

commit v1 on v0

--- a/solution.py
+++ b/solution.py
@@ -70,7 +70,12 @@
     new_queries = rotate(query_rows.reshape(shaped), positions).astype(jnp.bfloat16)
     new_keys = rotate(key_rows.reshape(shaped), positions).astype(jnp.bfloat16)
     new_values = value_rows.reshape(shaped).astype(jnp.bfloat16)
-    every_query = lax.all_gather(new_queries, "seq", axis=2, tiled=True)
+
+    def domain_press(array_here):
+        outer = jnp.concatenate([array_here] * lax.axis_size("seq"), 2)
+        return lax.all_to_all(outer, "seq", 2, 2, tiled=True)
+
+    every_query = domain_press(new_queries)
     pages_here = key_cache.shape[0]
     page_ids = seq_place * pages_here + jnp.arange(pages_here, dtype=jnp.int32)
     table_slots = jnp.arange(page_table.shape[0], dtype=jnp.int32)

time: 920 us -> 885 us (0.962)
  waiting for transfers between devices: 487 us -> 441 us
    all_gather x1 -> x0, waiting for transfers between devices: 69.3 us -> none  [per_device(): every_query = lax.all_gather(new_queries, 'seq', axis=2, tiled=True)]
    all_gather x1, waiting for transfers between devices: 61.3 us -> 82.6 us  [per_device(): lax.all_gather(w_value, 'seq', axis=0, tiled=True)]
  transfers between devices with their start and end apart: 7 -> 7, of which waited for: 7 -> 6; matrix products, arithmetic and copies ran while one was open for 5% -> 5% of each run, Pallas kernels for 0% -> 0%
where the time goes in v1:
time: 885 us; the launch traced here: 884 us
  waiting for transfers between devices  441 us (50%)
  blocking collectives  276 us (31%)
  matrix products  64.7 us (7%)
  local copies, waits for them, and re-layouts  57.9 us (7%)
  other arithmetic  20.7 us (2%)
  between operations  15.2 us (2%)
    unnamed x1, blocking collectives  140 us
    pmax x1, blocking collectives, per_device(): overall = lax.pmax(row_peak, 'seq')  136 us
    reduce_scatter x1, waiting for transfers between devices, per_device(): lax.psum_scatter(row_out * rescale[..., None], 'seq', scatter_dimension=2...  84.5 us
    all_gather x1, waiting for transfers between devices, per_device(): lax.all_gather(w_value, 'seq', axis=0, tiled=True)  82.6 us
    all_gather x1, waiting for transfers between devices, per_device(): lax.all_gather(w_out, 'seq', axis=0, tiled=True)  80.7 us
    all_gather x1, waiting for transfers between devices, per_device(): lax.all_gather(w_key, 'seq', axis=0, tiled=True)  80.2 us
    all_gather x1, waiting for transfers between devices, per_device(): lax.all_gather(w_query, 'seq', axis=0, tiled=True)  74.5 us
    reduce_scatter x1, waiting for transfers between devices, per_device(): lax.psum_scatter(partial_value, 'head', scatter_dimension=1, tiled=True)  35.8 us
  transfers between devices with their start and end apart: 7, of which 6 were waited for; matrix products, arithmetic and copies ran while one was open for 5% of the time, Pallas kernels for 0%

profile of v1, /device:TPU:2, one launch (start us, length us, event | category | flops | bytes accessed | tf_op | source)
XLA Modules:
  0.0 883.7 jit_solution(5154911389480444128)
XLA Ops:
  13.3 80.2 %all-gather.7.cloned.1.call-done = bf16[5120,384]{1,0:T(8,128)(2,1)} async-done(((bf16[160,384]{1,0:T(8,128)(2,1)}), bf16[5120,384]{1,0:T(8,128)(2,1)}) %all-gather.7.cloned.1.call-update) | async-done | bytes 3932176 | tf_op jit(solution)/shard_map/all_gather | solution.py:57
  93.4 6.3 copy.103
  99.8 74.5 %all-gather.5.cloned.1.call-done = bf16[5120,384]{1,0:T(8,128)(2,1)} async-done(((bf16[160,384]{1,0:T(8,128)(2,1)}), bf16[5120,384]{1,0:T(8,128)(2,1)}) %all-gather.5.cloned.1.call-update) | async-done | bytes 3932176 | tf_op jit(solution)/shard_map/all_gather | solution.py:56
  174.3 6.4 copy.100
  180.7 3.5 fusion.59
  187.0 3.6 copy.101
  190.6 7.3 all-to-all-start
  205.4 82.6 %all-gather.9.cloned.1.call-done = bf16[5120,384]{1,0:T(8,128)(2,1)} async-done(((bf16[160,384]{1,0:T(8,128)(2,1)}), bf16[5120,384]{1,0:T(8,128)(2,1)}) %all-gather.9.cloned.1.call-update) | async-done | bytes 3932176 | tf_op jit(solution)/shard_map/all_gather | solution.py:58
  288.0 6.3 copy.105
  295.1 4.0 convolution_convert_fusion
  299.1 82.5 %while.16 = (s32[]{:T(128)}, f32[2,8,256,3]{2,1,3,0:T(8,128)}, f32[2,8,256,3]{2,1,3,0:T(8,128)}, f32[2,8,256,3,128]{4,2,3,1,0:T(8,128)}, s32[16]{0:T(128)S(1)}, ...) while((s32[]{:T(128)}, f32[2,8,256,3]{2,1,3,0:T(8,128)}, ...), condition=%wide.region_9.10_spmd.clone.clone, body=%wide.region_3.9_spmd.clone.clone.sunk | while | flops 1071998720 | bytes 102284000 | solution.py:149
  303.9 3.7 bitcast_reduce_fusion.2
  311.1 7.6 bitcast_multiply_fusion.4
  325.9 11.2 %fusion.103 = f32[1,8,256,3,128]{4,1,3,2,0:T(8,128)S(1)} fusion(f32[8,3,128,256]{2,0,1,3:T(8,128)} %copy.163, f32[16,256,3,128]{3,1,2,0:T(8,128)} %bitcast_multiply_fusion.4, f32[8,256,3]{0,2,1:T(4,128)} %copy.164, f32[8,256,3]{0,2,1:T(4,128)} %copy.165, s32[16]{0:T(128)S(1)} %get-tuple-element.354), kind=kOutput, calls=%fused_computation.19.clone.1 | convolution fusion | flops 153354496 | bytes 12632128 | tf_op jit(solution)/shard_map/while/body/eval_jaxpr/pr,pqhd->rqhd/dot_general | solution.py:121
  345.1 3.7 bitcast_reduce_fusion.2
  352.4 7.6 bitcast_multiply_fusion.4
  367.1 11.2 %fusion.103 = f32[1,8,256,3,128]{4,1,3,2,0:T(8,128)S(1)} fusion(f32[8,3,128,256]{2,0,1,3:T(8,128)} %copy.163, f32[16,256,3,128]{3,1,2,0:T(8,128)} %bitcast_multiply_fusion.4, f32[8,256,3]{0,2,1:T(4,128)} %copy.164, f32[8,256,3]{0,2,1:T(4,128)} %copy.165, s32[16]{0:T(128)S(1)} %get-tuple-element.354), kind=kOutput, calls=%fused_computation.19.clone.1 | convolution fusion | flops 153354496 | bytes 12632128 | tf_op jit(solution)/shard_map/while/body/eval_jaxpr/pr,pqhd->rqhd/dot_general | solution.py:121
  381.6 136.1 %pmax.7 = f32[2,8,256,3]{2,1,3,0:T(8,128)S(1)} all-reduce(f32[2,8,256,3]{2,1,3,0:T(8,128)} %get-tuple-element.72), channel_id=1, replica_groups=mesh['seq'=32,'head'=8] {'seq'}, use_global_device_ids=true, to_apply=%region_10.11 | all-reduce | flops 12288 | bytes 98304 | tf_op jit(solution)/shard_map/pmax | solution.py:150
  518.6 7.2 broadcast_multiply_fusion
  527.7 140.4 %all-reduce = f32[2,8,256,3]{2,1,3,0:T(8,128)S(1)} all-reduce(f32[2,8,256,3]{2,1,3,0:T(8,128)S(1)} %get-tuple-element.213), channel_id=3, replica_groups=mesh['seq'=32,'head'=8] {'seq'}, use_global_device_ids=true, to_apply=%region_12.13.clone | all-reduce | flops 12288 | bytes 98304
  668.2 84.5 %reduce-scatter.4.cloned.1.call-done = f32[2,8,8,3,128]{4,2,3,1,0:T(8,128)} async-done(((f32[2,8,256,3,128]{4,2,3,1,0:T(8,128)}), f32[2,8,8,3,128]{4,2,3,1,0:T(8,128)}) %reduce-scatter.4.cloned.1.call-update) | async-done | bytes 196624 | tf_op jit(solution)/shard_map/reduce_scatter | solution.py:153
  753.7 80.7 %all-gather.11.cloned.1.call-done = bf16[5120,384]{1,0:T(8,128)(2,1)} async-done(((bf16[160,384]{1,0:T(8,128)(2,1)}), bf16[5120,384]{1,0:T(8,128)(2,1)}) %all-gather.11.cloned.1.call-update) | async-done | bytes 3932176 | tf_op jit(solution)/shard_map/all_gather | solution.py:59
  834.4 5.0 fusion.66
  839.4 35.8 %reduce-scatter.6.cloned.1.call-done = f32[128,640]{1,0:T(8,128)} async-done(((f32[128,5120]{1,0:T(8,128)}), f32[128,640]{1,0:T(8,128)}) %reduce-scatter.6.cloned.1.call-update) | async-done | bytes 327696 | tf_op jit(solution)/shard_map/reduce_scatter | solution.py:162
  (157 shorter events, 58.7 us)
Async XLA Ops:
  7.2 5.8 copy-start.10
  7.2 86.2 %all-gather.7.cloned.1.call-start = ((), (), s32[]{:S(2)}) async-start(), calls=%async_computation.4 | async-start | bytes 4055040 | tf_op jit(solution)/shard_map/all_gather | solution.py:57
  7.9 166.4 %all-gather.5.cloned.1.call-start = ((), (), s32[]{:S(2)}) async-start(), calls=%async_computation.3 | async-start | bytes 4055040 | tf_op jit(solution)/shard_map/all_gather | solution.py:56
  8.7 279.4 %all-gather.9.cloned.1.call-start = ((), (), s32[]{:S(2)}) async-start(), calls=%async_computation.5 | async-start | bytes 4055040 | tf_op jit(solution)/shard_map/all_gather | solution.py:58
  174.3 6.4 copy-start.2
  174.3 6.4 copy-start.9
  180.7 3.5 copy-start.1
  190.6 108.5 %all-to-all-start = ((bf16[2,8,256,3,128]{4,1,3,0,2:T(8,128)(2,1)}), bf16[2,8,256,3,128]{4,1,3,0,2:T(8,128)(2,1)}, u32[]{:S(2)}, u32[]{:S(2)}) async-start(bf16[2,8,256,3,128]{4,1,3,0,2:T(8,128)(2,1)} %copy.101), calls=%async_computation | async-start | bytes 6291456 | tf_op jit(solution)/shard_map/all_to_all | solution.py:76
  198.0 554.7 %reduce-scatter.4.cloned.1.call-start = ((), (), s32[]{:S(2)}) async-start(), calls=%async_computation.6 | async-start | bytes 6488064 | tf_op jit(solution)/shard_map/reduce_scatter | solution.py:153
  201.6 3.6 copy-start.8
  307.6 2.6 copy-start
  311.1 7.6 copy-start.3
  337.1 2.3 copy-start.6
  337.1 2.5 copy-start.4
  339.7 0.6 copy-start.7
  339.7 0.6 copy-start.5
  348.8 2.6 copy-start
  352.3 7.6 copy-start.3
  378.3 2.4 copy-start.6
  378.3 2.6 copy-start.4
  380.9 0.6 copy-start.7
  525.8 0.7 copy-start.11
  525.8 308.6 %all-gather.11.cloned.1.call-start = ((), (), s32[]{:S(2)}) async-start(), calls=%async_computation.7 | async-start | bytes 4055040 | tf_op jit(solution)/shard_map/all_gather | solution.py:59
  526.4 348.8 %reduce-scatter.6.cloned.1.call-start = ((), (), s32[]{:S(2)}) async-start(), calls=%async_computation.8 | async-start | bytes 2949120 | tf_op jit(solution)/shard_map/reduce_scatter | solution.py:162
  (1 other events, 0.6 us)
Sparse Core Ops, SparseCore 0:
  10.6 82.7 all-gather.6
  96.0 78.2 all-gather.4
  176.9 111.1 all-gather.8
  526.0 226.6 reduce-scatter.3
  755.4 78.9 all-gather.10
  839.5 35.6 reduce-scatter.5
